TPU v7x, 32 devices: a whole 2x2x4 slice. The times are simulated.
32 devices in a mesh: segment: 4 (over y, x), seq: 8 (over z, core).
Axes of the slice: x: 2, y: 2, z: 4, core: 2. Of those that a mesh axis runs over, the one named last changes fastest.
Arguments:
- hidden: bfloat16 [4, 8192, 8192], P('segment', 'seq'), may hold values from -6 to 6
- span_lengths: int32 [4, 64], replicated, may hold values from 1 to 512, 8192 in all within a row
- section_of: int32 [4, 64], replicated, may hold values from 0 to 31
- section_live: int32 [32], P('seq'), may hold values 0 or 1
- w_in: bfloat16 [8192, 2048], P('seq'), may hold values from -0.5 to 0.5
- norm_gain: float32 [2048], replicated, may hold values from 0.5 to 1.5
- w_query: bfloat16 [2048, 2048], P(None, 'segment'), may hold values from -0.125 to 0.125
- w_key: bfloat16 [2048, 2048], P(None, 'segment'), may hold values from -0.125 to 0.125
- w_value: bfloat16 [2048, 2048], P(None, 'segment'), may hold values from -0.125 to 0.125
- w_out: bfloat16 [2048, 2048], P('segment'), may hold values from -0.125 to 0.125
Outputs:
- section_out: bfloat16 [32, 2048], P('seq')
All inputs are finite; a program needn't handle non-finite values. No bound on the sum of `section_live` on one device may be relied on, other than what follows from the above.
Results may differ from a plain program's by a relative error of at most 0.007.
Values may be sent and summed in bfloat16 or wider, within the bound.
A program may use at most 128 MiB of HBM per device.

v0:
```python
import jax
import jax.numpy as jnp
from jax import lax
from jax.sharding import PartitionSpec as P

HEAD_DIM = 128


def shards(
    hidden, span_lengths, section_of, section_live, w_in, norm_gain, w_query, w_key, w_value, w_out
):
    tokens = hidden[0]
    seq_count = lax.axis_size("seq")
    seq_index = lax.axis_index("seq")
    segment_index = lax.axis_index("segment")
    tok_count = tokens.shape[0]
    lengths = lax.dynamic_index_in_dim(span_lengths, segment_index, 0, keepdims=False)
    span_ends = jnp.cumsum(lengths)
    span_starts = span_ends - lengths
    positions = seq_index * tok_count + jnp.arange(tok_count, dtype=jnp.int32)
    member = (
        (positions[None, :] >= span_starts[:, None]) & (positions[None, :] < span_ends[:, None])
    ).astype(jnp.bfloat16)
    partial_value = jnp.dot(member, tokens, preferred_element_type=jnp.float32)
    length_float = lengths.astype(jnp.float32)
    sections_here = section_live.shape[0]
    section_total = sections_here * seq_count
    section_ids = jnp.arange(section_total, dtype=jnp.int32)
    own_sections = seq_index * sections_here + jnp.arange(sections_here, dtype=jnp.int32)
    flat_sections = section_of.reshape(-1)
    count_all = jnp.sum(
        (section_ids[:, None] == flat_sections[None, :]).astype(jnp.float32), axis=1
    )
    doc_sections = lax.dynamic_index_in_dim(section_of, segment_index, 0, keepdims=False)
    weighted = partial_value / length_float[:, None]
    doc_onehot = (section_ids[:, None] == doc_sections[None, :]).astype(jnp.float32)
    section_part = jnp.dot(doc_onehot, weighted, precision=lax.Precision.HIGHEST)
    feature_block = lax.psum_scatter(section_part, "seq", scatter_dimension=1, tiled=True)
    doc_total = lax.psum(feature_block, "segment")
    pooled = (doc_total / jnp.maximum(count_all, 1.0)[:, None]).astype(jnp.bfloat16)
    projected = jnp.dot(pooled, w_in, preferred_element_type=jnp.float32)
    section_in = lax.psum_scatter(projected, "seq", scatter_dimension=0, tiled=True)
    scale = lax.rsqrt(jnp.mean(section_in * section_in, axis=1, keepdims=True) + 1e-05)
    normed = (section_in * scale * norm_gain[None, :]).astype(jnp.bfloat16)
    queries = jnp.dot(normed, w_query, preferred_element_type=jnp.float32).astype(jnp.bfloat16)
    keys_here = jnp.dot(normed, w_key, preferred_element_type=jnp.float32).astype(jnp.bfloat16)
    values_here = jnp.dot(normed, w_value, preferred_element_type=jnp.float32).astype(jnp.bfloat16)
    live_here = section_live.astype(jnp.bfloat16)
    keys_all, values_all, live_all = (
        lax.all_gather(keys_here, "seq", axis=0, tiled=True),
        lax.all_gather(values_here, "seq", axis=0, tiled=True),
        lax.all_gather(live_here, "seq", axis=0, tiled=True),
    )
    local_heads = queries.shape[1] // HEAD_DIM
    query_heads = queries.reshape(sections_here, local_heads, HEAD_DIM)
    key_heads = keys_all.reshape(section_total, local_heads, HEAD_DIM)
    value_heads = values_all.reshape(section_total, local_heads, HEAD_DIM)
    scores = jnp.einsum("qhd,khd->hqk", query_heads, key_heads, preferred_element_type=jnp.float32)
    scores = scores / jnp.sqrt(jnp.float32(HEAD_DIM))
    allowed = (live_all[None, :] > 0) | (section_ids[None, :] == own_sections[:, None])
    scores = jnp.where(allowed[None, :, :], scores, jnp.float32(-1e30))
    probs = jax.nn.softmax(scores, axis=-1).astype(jnp.bfloat16)
    attended = jnp.einsum(
        "hqk,khd->qhd", probs, value_heads, preferred_element_type=jnp.float32
    ).astype(jnp.bfloat16)
    attended = attended.reshape(sections_here, local_heads * HEAD_DIM)
    head_terms = jnp.dot(attended, w_out, preferred_element_type=jnp.float32)
    combined = lax.psum(head_terms, "segment")
    return (section_in + combined).astype(jnp.bfloat16)


def solution(mesh):
    in_specs = (
        P("segment", "seq", None),
        P(),
        P(),
        P("seq"),
        P("seq", None),
        P(),
        P(None, "segment"),
        P(None, "segment"),
        P(None, "segment"),
        P("segment", None),
    )
    out_specs = P("seq", None)
    return jax.shard_map(shards, mesh=mesh, in_specs=in_specs, out_specs=out_specs, check_vma=False)
```

profile of v0, /device:TPU:0, one launch (start us, length us, event | category | flops | bytes accessed | tf_op | source)
XLA Modules:
  0.0 217.7 jit_solution(10877947771555918930)
XLA Ops:
  6.5 0.9 fusion.30
  7.4 0.1 copy.25
  7.6 0.1 reduce
  7.7 0.7 bitcast_subtract_fusion
  8.4 8.8 %fusion.3 = f32[64,8192]{1,0:T(8,128)S(1)} fusion(bf16[1,1024,8192]{2,1,0:T(8,128)(2,1)} %param.10, f32[64]{0:T(128)S(1)} %get-tuple-element.6, s32[1024]{0:T(1024)S(1)} %iota_add_fusion, s32[64]{0:T(128)S(1)} %reduce, s32[64]{0:T(128)S(1)} %bitcast_subtract_fusion), kind=kOutput, calls=%fused_computation.3 | convolution fusion | flops 1074462720 | bytes 18879232 | tf_op jit(solution)/shard_map/dot_general | solution.py:24
  17.3 1.8 fusion.25
  19.3 0.7 fusion.31
  20.6 0.2 dynamic-update-slice
  20.9 18.2 %all-reduce = bf16[32]{0:T(256)(128)(2,1)S(1)} all-reduce(bf16[32]{0:T(256)(128)(2,1)S(1)} %dynamic-update-slice), channel_id=1, replica_groups=mesh['segment'=4,'seq'=8] {'seq'}, use_global_device_ids=true, to_apply=%add | all-reduce | flops 32 | bytes 128
  39.1 0.1 convert_reduce_fusion
  39.2 15.9 %reduce-scatter.2.cloned.1.call-done = f32[32,1024]{1,0:T(8,128)} async-done(((f32[32,8192]{1,0:T(8,128)}), f32[32,1024]{1,0:T(8,128)}) %reduce-scatter.2.cloned.1.call-update) | async-done | bytes 131088 | tf_op jit(solution)/shard_map/reduce_scatter | solution.py:38
  55.8 42.1 %all-reduce.5.cloned.1.call-done = f32[32,1024]{1,0:T(8,128)} async-done(((f32[32,1024]{1,0:T(8,128)}), f32[32,1024]{1,0:T(8,128)}) %all-reduce.5.cloned.1.call-update) | async-done | bytes 131088 | tf_op jit(solution)/shard_map/psum | solution.py:39
  97.9 3.8 %fusion.20 = f32[32,2048]{1,0:T(8,128)} fusion(bf16[1024,2048]{1,0:T(8,128)(2,1)} %param.14, f32[32,1024]{1,0:T(8,128)} %all-reduce.5.cloned.1.call-done, f32[32]{0:T(128)S(1)} %broadcast_maximum_fusion), kind=kOutput, calls=%fused_computation.24 | convolution fusion | flops 134283264 | bytes 4587648 | tf_op jit(solution)/shard_map/dot_general | solution.py:41
  101.8 55.5 %all-reduce.7.cloned.1.call-done = f32[32,2048]{1,0:T(8,128)} async-done(((f32[32,2048]{1,0:T(8,128)}), f32[32,2048]{1,0:T(8,128)}) %all-reduce.7.cloned.1.call-update) | async-done | bytes 262160
  157.3 1.0 multiply_reduce_fusion
  158.3 2.0 fusion.11
  160.3 14.1 %all-gather.1 = bf16[8,4,512]{2,1,0:T(4,128)(2,1)S(1)} all-gather(bf16[1,4,512]{2,1,0:T(4,128)(2,1)S(1)} %fusion.11), channel_id=1, replica_groups=mesh['segment'=4,'seq'=8] {'seq'}, dimensions={0}, use_global_device_ids=true | all-gather | bytes 36864 | tf_op jit(solution)/shard_map/all_gather | solution.py:50
  174.4 2.2 fusion.8
  176.6 0.2 fusion.32
  176.8 2.1 fusion.9
  178.8 14.1 %all-gather = bf16[8,4,512]{2,1,0:T(4,128)(2,1)S(1)} all-gather(bf16[1,4,512]{2,1,0:T(4,128)(2,1)S(1)} %fusion.9), channel_id=1, replica_groups=mesh['segment'=4,'seq'=8] {'seq'}, dimensions={0}, use_global_device_ids=true | all-gather | bytes 36864 | tf_op jit(solution)/shard_map/all_gather | solution.py:51
  193.0 0.5 fusion.13
  193.5 16.2 %psum.15 = f32[4,2048]{1,0:T(4,128)S(1)} all-reduce(f32[4,2048]{1,0:T(4,128)S(1)} %fusion.13), channel_id=1, replica_groups=mesh['segment'=4,'seq'=8] {'segment'}, use_global_device_ids=true, to_apply=%region_8.9 | all-reduce | flops 8192 | bytes 65536 | tf_op jit(solution)/shard_map/psum | solution.py:68
  209.7 1.5 add_convert_fusion
  (28 shorter events, 0.5 us)
Async XLA Ops:
  6.5 186.4 %copy-start = (bf16[512,2048]{1,0:T(8,128)(2,1)S(1)}, bf16[512,2048]{1,0:T(8,128)(2,1)}, u32[]{:S(2)}) copy-start(bf16[512,2048]{1,0:T(8,128)(2,1)} %param.19) | copy-start | bytes 6291460
  6.5 48.5 %reduce-scatter.2.cloned.1.call-start = ((), (), s32[]{:S(2)}) async-start(), calls=%async_computation.1 | async-start | bytes 1179648 | tf_op jit(solution)/shard_map/reduce_scatter | solution.py:38
  17.3 1.9 copy-start.2
  17.3 2.0 copy-start.4
  17.3 2.0 copy-start.3
  19.1 78.7 %all-reduce.5.cloned.1.call-start = ((), (), s32[]{:S(2)}) async-start(), calls=%async_computation.2 | async-start | bytes 262144 | tf_op jit(solution)/shard_map/psum | solution.py:39
  55.1 102.2 %all-reduce.7.cloned.1.call-start = ((), (), s32[]{:S(2)}) async-start(), calls=%async_computation.3 | async-start | bytes 524288
  55.8 102.5 %copy-start.1 = (f32[2048]{0:T(1024)S(1)}, f32[2048]{0:T(1024)}, u32[]{:S(2)}) copy-start(f32[2048]{0:T(1024)} %param.15) | copy-start | bytes 24580
Sparse Core Ops, SparseCore 0:
  19.3 35.7 reduce-scatter.1
  58.0 39.8 all-reduce.4
  101.9 55.4 all-reduce.6
where the time goes:
time: 218 us
  waiting for transfers between devices  113 us (52%)
  blocking collectives  62.6 us (29%)
  matrix products  21.3 us (10%)
  between operations  14.5 us (7%)
  other arithmetic  4.58 us (2%)
    unnamed x4, waiting for transfers between devices  55.5 us
    psum x1, waiting for transfers between devices, shards(): doc_total = lax.psum(feature_block, 'segment')  42.1 us
    unnamed x1, blocking collectives  18.2 us
    psum x1, blocking collectives, shards(): combined = lax.psum(head_terms, 'segment')  16.2 us
    reduce_scatter x1, waiting for transfers between devices, shards(): lax.psum_scatter(section_part, 'seq', scatter_dimension=1, tiled=True)  15.9 us
    all_gather x1, blocking collectives, shards(): lax.all_gather(keys_here, 'seq', axis=0, tiled=True)  14.1 us
    all_gather x1, blocking collectives, shards(): lax.all_gather(values_here, 'seq', axis=0, tiled=True)  14.1 us
    dot_general x1, matrix products, shards(): partial_value = jnp.dot(member, tokens, preferred_element_type=jnp.float32)  8.85 us
  transfers between devices with their start and end apart: 3, of which 3 were waited for; matrix products, arithmetic and copies ran while one was open for 1% of the time, Pallas kernels for 0%

commit v1 on v0

--- a/solution.py
+++ b/solution.py
@@ -1,9 +1,37 @@
+import functools
 import jax
 import jax.numpy as jnp
 from jax import lax
 from jax.sharding import PartitionSpec as P
+from jax.lax import axis_index, axis_size, ppermute
 
 HEAD_DIM = 128
+
+
+def _clear_spot(point, dim_no):
+    z2, big, far_arr = (axis_size("seq"), axis_index("seq"), point.shape[dim_no])
+    grid = [(hop_no, (hop_no + 1) % z2) for hop_no in range(z2)]
+    so_far_all = [(hop_no, (hop_no - 1) % z2) for hop_no in range(z2)]
+    w_next = jnp.zeros(
+        (*point.shape[:dim_no], z2 * far_arr, *point.shape[dim_no + 1 :]), point.dtype
+    )
+    top = arr_out = point
+    w_next = lax.dynamic_update_slice_in_dim(w_next, point, big * far_arr, axis=dim_no)
+    n_now = z2 // 2
+    for num in range(1, n_now + 1):
+        top = ppermute(top, axis_name="seq", perm=grid)
+        w_next = lax.dynamic_update_slice_in_dim(
+            w_next, top, (big - num) % z2 * far_arr, axis=dim_no
+        )
+        if num < z2 - n_now:
+            arr_out = ppermute(arr_out, axis_name="seq", perm=so_far_all)
+            w_next = lax.dynamic_update_slice_in_dim(
+                w_next, arr_out, (big + num) % z2 * far_arr, axis=dim_no
+            )
+    return w_next
+
+
+fit_fields = functools.partial(_clear_spot, dim_no=0)
 
 
 def shards(
@@ -47,7 +75,7 @@
     values_here = jnp.dot(normed, w_value, preferred_element_type=jnp.float32).astype(jnp.bfloat16)
     live_here = section_live.astype(jnp.bfloat16)
     keys_all, values_all, live_all = (
-        lax.all_gather(keys_here, "seq", axis=0, tiled=True),
+        fit_fields(keys_here),
         lax.all_gather(values_here, "seq", axis=0, tiled=True),
         lax.all_gather(live_here, "seq", axis=0, tiled=True),
     )

time: 218 us -> 222 us (1.018)
  blocking collectives: 62.6 us -> 48.6 us
  starting transfers between devices: 0.08 us -> 10.7 us
  waiting for transfers between devices: 113 us -> 121 us
    all_gather x1 -> x0, blocking collectives: 14.1 us -> none  [shards(): lax.all_gather(keys_here, 'seq', axis=0, tiled=True)]
    ppermute x0 -> x7, starting transfers between devices: none -> 10.6 us  [the longest x3 10.2 us: _clear_spot(): arr_out = ppermute(arr_out, axis_name='seq', perm=so_far_all)]
    ppermute x0 -> x7, waiting for transfers between devices: none -> 7.37 us  [the longest x4 7.3 us: _clear_spot(): top = ppermute(top, axis_name='seq', perm=grid)]
  transfers between devices with their start and end apart: 3 -> 10, of which waited for: 3 -> 6; matrix products, arithmetic and copies ran while one was open for 1% -> 1% of each run, Pallas kernels for 0% -> 0%
where the time goes in v1:
time: 222 us
  waiting for transfers between devices  121 us (55%)
  blocking collectives  48.6 us (22%)
  matrix products  21.3 us (10%)
  between operations  14.7 us (7%)
  starting transfers between devices  10.7 us (5%)
  other arithmetic  4.73 us (2%)
    unnamed x4, waiting for transfers between devices  55.5 us
    psum x1, waiting for transfers between devices, shards(): doc_total = lax.psum(feature_block, 'segment')  41.9 us
    unnamed x1, blocking collectives  18.2 us
    psum x1, blocking collectives, shards(): combined = lax.psum(head_terms, 'segment')  16.3 us
    reduce_scatter x1, waiting for transfers between devices, shards(): lax.psum_scatter(section_part, 'seq', scatter_dimension=1, tiled=True)  15.9 us
    all_gather x1, blocking collectives, shards(): lax.all_gather(values_here, 'seq', axis=0, tiled=True)  14.1 us
    ppermute x3, starting transfers between devices, _clear_spot(): arr_out = ppermute(arr_out, axis_name='seq', perm=so_far_all)  10.2 us
    dot_general x1, matrix products, shards(): partial_value = jnp.dot(member, tokens, preferred_element_type=jnp.float32)  8.85 us
  transfers between devices with their start and end apart: 10, of which 6 were waited for; matrix products, arithmetic and copies ran while one was open for 1% of the time, Pallas kernels for 0%

profile of v1, /device:TPU:0, one launch (start us, length us, event | category | flops | bytes accessed | tf_op | source)
XLA Modules:
  0.0 222.0 jit_solution(16816890030447267579)
XLA Ops:
  6.5 0.9 fusion.31
  7.7 0.7 bitcast_subtract_fusion
  8.4 8.8 %fusion.3 = f32[64,8192]{1,0:T(8,128)S(1)} fusion(bf16[1,1024,8192]{2,1,0:T(8,128)(2,1)} %param.10, f32[64]{0:T(128)S(1)} %get-tuple-element.6, s32[1024]{0:T(1024)S(1)} %iota_add_fusion, s32[64]{0:T(128)S(1)} %reduce, s32[64]{0:T(128)S(1)} %bitcast_subtract_fusion), kind=kOutput, calls=%fused_computation.3 | convolution fusion | flops 1074462720 | bytes 18879232 | tf_op jit(solution)/shard_map/dot_general | solution.py:52
  17.3 1.8 fusion.25
  19.3 0.7 fusion.32
  20.9 18.2 %all-reduce = bf16[32]{0:T(256)(128)(2,1)S(1)} all-reduce(bf16[32]{0:T(256)(128)(2,1)S(1)} %dynamic-update-slice), channel_id=1, replica_groups=mesh['segment'=4,'seq'=8] {'seq'}, use_global_device_ids=true, to_apply=%add | all-reduce | flops 32 | bytes 128
  39.2 15.9 %reduce-scatter.2.cloned.1.call-done = f32[32,1024]{1,0:T(8,128)} async-done(((f32[32,8192]{1,0:T(8,128)}), f32[32,1024]{1,0:T(8,128)}) %reduce-scatter.2.cloned.1.call-update) | async-done | bytes 131088 | tf_op jit(solution)/shard_map/reduce_scatter | solution.py:66
  56.0 41.9 %all-reduce.5.cloned.1.call-done = f32[32,1024]{1,0:T(8,128)} async-done(((f32[32,1024]{1,0:T(8,128)}), f32[32,1024]{1,0:T(8,128)}) %all-reduce.5.cloned.1.call-update) | async-done | bytes 131088 | tf_op jit(solution)/shard_map/psum | solution.py:67
  97.9 3.8 %fusion.19 = f32[32,2048]{1,0:T(8,128)} fusion(bf16[1024,2048]{1,0:T(8,128)(2,1)} %param.14, f32[32,1024]{1,0:T(8,128)} %all-reduce.5.cloned.1.call-done, f32[32]{0:T(128)S(1)} %broadcast_maximum_fusion), kind=kOutput, calls=%fused_computation.23 | convolution fusion | flops 134283264 | bytes 4587648 | tf_op jit(solution)/shard_map/dot_general | solution.py:69
  101.8 55.5 %all-reduce.7.cloned.1.call-done = f32[32,2048]{1,0:T(8,128)} async-done(((f32[32,2048]{1,0:T(8,128)}), f32[32,2048]{1,0:T(8,128)}) %all-reduce.7.cloned.1.call-update) | async-done | bytes 262160
  157.3 1.1 multiply_reduce_fusion
  158.5 1.3 constant_dynamic-update-slice_fusion.7
  159.7 3.5 %collective-permute-start.1 = (bf16[4,512]{1,0:T(4,128)(2,1)S(1)}, bf16[4,512]{1,0:T(4,128)(2,1)S(1)}, u32[]{:S(2)}, u32[]{:S(2)}) collective-permute-start(bf16[4,512]{1,0:T(4,128)(2,1)S(1)} %get-tuple-element.10), channel_id=1, source_target_pairs={{0,7},{1,0},{2,1},{3,2},{4,3},{5,4},{6,5},{7,6},{8,15},{9,8},{10,9... | collective-permute-start | bytes 12296 | tf_op jit(solution)/shard_map/ppermute | solution.py:27
  163.3 1.3 fusion.9
  164.5 14.1 %all-gather = bf16[8,4,512]{2,1,0:T(4,128)(2,1)S(1)} all-gather(bf16[1,4,512]{2,1,0:T(4,128)(2,1)S(1)} %fusion.9), channel_id=1, replica_groups=mesh['segment'=4,'seq'=8] {'seq'}, dimensions={0}, use_global_device_ids=true | all-gather | bytes 36864 | tf_op jit(solution)/shard_map/all_gather | solution.py:79
  179.1 3.2 %collective-permute-start.3 = (bf16[4,512]{1,0:T(4,128)(2,1)S(1)}, bf16[4,512]{1,0:T(4,128)(2,1)S(1)}, u32[]{:S(2)}, u32[]{:S(2)}) collective-permute-start(bf16[4,512]{1,0:T(4,128)(2,1)S(1)} %collective-permute-done.1), channel_id=1, source_target_pairs={{0,7},{1,0},{2,1},{3,2},{4,3},{5,4},{6,5},{7,6},{8,15},{9,8},{10,9... | collective-permute-start | bytes 12296 | tf_op jit(solution)/shard_map/ppermute | solution.py:27
  182.3 1.3 collective-permute-done.2
  183.6 3.5 %collective-permute-start.5 = (bf16[4,512]{1,0:T(4,128)(2,1)S(1)}, bf16[4,512]{1,0:T(4,128)(2,1)S(1)}, u32[]{:S(2)}, u32[]{:S(2)}) collective-permute-start(bf16[4,512]{1,0:T(4,128)(2,1)S(1)} %collective-permute-done.3), channel_id=1, source_target_pairs={{0,7},{1,0},{2,1},{3,2},{4,3},{5,4},{6,5},{7,6},{8,15},{9,8},{10,9... | collective-permute-start | bytes 12296 | tf_op jit(solution)/shard_map/ppermute | solution.py:27
  187.1 1.3 collective-permute-done.4
  188.4 4.8 %collective-permute-done.6 = bf16[4,512]{1,0:T(4,128)(2,1)S(1)} collective-permute-done((bf16[4,512]{1,0:T(4,128)(2,1)S(1)}, bf16[4,512]{1,0:T(4,128)(2,1)S(1)}, u32[]{:S(2)}, u32[]{:S(2)}) %collective-permute-start.6) | collective-permute-done | bytes 4128 | tf_op jit(solution)/shard_map/ppermute | solution.py:22
  193.2 2.2 fusion.8
  195.5 2.2 fusion.12
  197.7 16.3 %psum.15 = f32[4,2048]{1,0:T(4,128)S(1)} all-reduce(f32[4,2048]{1,0:T(4,128)S(1)} %fusion.12), channel_id=1, replica_groups=mesh['segment'=4,'seq'=8] {'segment'}, use_global_device_ids=true, to_apply=%region_8.9 | all-reduce | flops 8192 | bytes 65536 | tf_op jit(solution)/shard_map/psum | solution.py:96
  214.0 1.5 add_convert_fusion
  (50 shorter events, 1.8 us)
Async XLA Ops:
  6.5 151.9 %copy-start = (bf16[2048,512]{1,0:T(8,128)(2,1)S(1)}, bf16[2048,512]{1,0:T(8,128)(2,1)}, u32[]{:S(2)}) copy-start(bf16[2048,512]{1,0:T(8,128)(2,1)} %param.17) | copy-start | bytes 6291460
  6.5 48.5 %reduce-scatter.2.cloned.1.call-start = ((), (), s32[]{:S(2)}) async-start(), calls=%async_computation.1 | async-start | bytes 1179648 | tf_op jit(solution)/shard_map/reduce_scatter | solution.py:66
  17.3 1.9 copy-start.3
  17.3 2.0 copy-start.5
  17.3 2.0 copy-start.4
  19.1 78.7 %all-reduce.5.cloned.1.call-start = ((), (), s32[]{:S(2)}) async-start(), calls=%async_computation.2 | async-start | bytes 262144 | tf_op jit(solution)/shard_map/psum | solution.py:67
  55.1 102.2 %all-reduce.7.cloned.1.call-start = ((), (), s32[]{:S(2)}) async-start(), calls=%async_computation.3 | async-start | bytes 524288
  55.9 102.5 %copy-start.2 = (f32[2048]{0:T(1024)S(1)}, f32[2048]{0:T(1024)}, u32[]{:S(2)}) copy-start(f32[2048]{0:T(1024)} %param.15) | copy-start | bytes 24580
  157.3 6.0 %copy-start.1 = (bf16[2048,512]{1,0:T(8,128)(2,1)S(1)}, bf16[2048,512]{1,0:T(8,128)(2,1)}, u32[]{:S(2)}) copy-start(bf16[2048,512]{1,0:T(8,128)(2,1)} %param.18) | copy-start | bytes 6291460
  159.7 18.9 %collective-permute-start = (bf16[4,512]{1,0:T(4,128)(2,1)S(1)}, bf16[4,512]{1,0:T(4,128)(2,1)S(1)}, u32[]{:S(2)}, u32[]{:S(2)}) collective-permute-start(bf16[4,512]{1,0:T(4,128)(2,1)S(1)} %get-tuple-element.10), channel_id=1, source_target_pairs={{0,1},{1,2},{2,3},{3,4},{4,5},{5,6},{6,7},{7,0},{8,9},{9,10},{10,1... | collective-permute-start | bytes 12296 | tf_op jit(solution)/shard_map/ppermute | solution.py:22
  159.7 19.3 %collective-permute-start.1 = (bf16[4,512]{1,0:T(4,128)(2,1)S(1)}, bf16[4,512]{1,0:T(4,128)(2,1)S(1)}, u32[]{:S(2)}, u32[]{:S(2)}) collective-permute-start(bf16[4,512]{1,0:T(4,128)(2,1)S(1)} %get-tuple-element.10), channel_id=1, source_target_pairs={{0,7},{1,0},{2,1},{3,2},{4,3},{5,4},{6,5},{7,6},{8,15},{9,8},{10,9... | collective-permute-start | bytes 12296 | tf_op jit(solution)/shard_map/ppermute | solution.py:27
  178.7 4.9 %collective-permute-start.2 = (bf16[4,512]{1,0:T(4,128)(2,1)S(1)}, bf16[4,512]{1,0:T(4,128)(2,1)S(1)}, u32[]{:S(2)}, u32[]{:S(2)}) collective-permute-start(bf16[4,512]{1,0:T(4,128)(2,1)S(1)} %collective-permute-done), channel_id=1, source_target_pairs={{0,1},{1,2},{2,3},{3,4},{4,5},{5,6},{6,7},{7,0},{8,9},{9,10},{10,1... | collective-permute-start | bytes 12296 | tf_op jit(solution)/shard_map/ppermute | solution.py:22
  179.1 4.5 %collective-permute-start.3 = (bf16[4,512]{1,0:T(4,128)(2,1)S(1)}, bf16[4,512]{1,0:T(4,128)(2,1)S(1)}, u32[]{:S(2)}, u32[]{:S(2)}) collective-permute-start(bf16[4,512]{1,0:T(4,128)(2,1)S(1)} %collective-permute-done.1), channel_id=1, source_target_pairs={{0,7},{1,0},{2,1},{3,2},{4,3},{5,4},{6,5},{7,6},{8,15},{9,8},{10,9... | collective-permute-start | bytes 12296 | tf_op jit(solution)/shard_map/ppermute | solution.py:27
  183.5 4.8 %collective-permute-start.4 = (bf16[4,512]{1,0:T(4,128)(2,1)S(1)}, bf16[4,512]{1,0:T(4,128)(2,1)S(1)}, u32[]{:S(2)}, u32[]{:S(2)}) collective-permute-start(bf16[4,512]{1,0:T(4,128)(2,1)S(1)} %collective-permute-done.2), channel_id=1, source_target_pairs={{0,1},{1,2},{2,3},{3,4},{4,5},{5,6},{6,7},{7,0},{8,9},{9,10},{10,1... | collective-permute-start | bytes 12296 | tf_op jit(solution)/shard_map/ppermute | solution.py:22
  183.6 4.8 %collective-permute-start.5 = (bf16[4,512]{1,0:T(4,128)(2,1)S(1)}, bf16[4,512]{1,0:T(4,128)(2,1)S(1)}, u32[]{:S(2)}, u32[]{:S(2)}) collective-permute-start(bf16[4,512]{1,0:T(4,128)(2,1)S(1)} %collective-permute-done.3), channel_id=1, source_target_pairs={{0,7},{1,0},{2,1},{3,2},{4,3},{5,4},{6,5},{7,6},{8,15},{9,8},{10,9... | collective-permute-start | bytes 12296 | tf_op jit(solution)/shard_map/ppermute | solution.py:27
  188.4 4.8 %collective-permute-start.6 = (bf16[4,512]{1,0:T(4,128)(2,1)S(1)}, bf16[4,512]{1,0:T(4,128)(2,1)S(1)}, u32[]{:S(2)}, u32[]{:S(2)}) collective-permute-start(bf16[4,512]{1,0:T(4,128)(2,1)S(1)} %collective-permute-done.4), channel_id=1, source_target_pairs={{0,1},{1,2},{2,3},{3,4},{4,5},{5,6},{6,7},{7,0},{8,9},{9,10},{10,1... | collective-permute-start | bytes 12296 | tf_op jit(solution)/shard_map/ppermute | solution.py:22
Sparse Core Ops, SparseCore 0:
  19.3 35.7 reduce-scatter.1
  58.0 39.8 all-reduce.4
  101.9 55.4 all-reduce.6
